TPU v7x, 256 devices: a whole 4x4x8 slice. The times are simulated.
256 devices in a mesh: ha: 16 (over x, y_hi, core), wa: 16 (over z, y_lo).
Axes of the slice: x: 4, y: 4 (y_hi: 2, y_lo: 2; y = y_hi * 2 + y_lo), z: 8, core: 2. Of those that a mesh axis runs over, the one named last changes fastest.
Arguments:
- tokens: bfloat16 [256, 256, 256], P('ha', 'wa'), may hold values from -6 to 6
- gain_attn: float32 [256], replicated, may hold values from 0.25 to 1.75
- qkv_fine: bfloat16 [256, 768], replicated, may hold values from -0.375 to 0.375
- scale_fine: float32 [4], replicated, may hold values from 2 to 24
- out_fine: bfloat16 [256, 256], replicated, may hold values from -0.375 to 0.375
- gain_ffn: float32 [256], replicated, may hold values from 0.25 to 1.75
- ffn_in: bfloat16 [256, 1536], replicated, may hold values from -0.375 to 0.375
- ffn_out: bfloat16 [768, 256], replicated, may hold values from -0.21875 to 0.21875
- up_proj: bfloat16 [256, 1024], replicated, may hold values from -0.375 to 0.375
- gain_coarse: float32 [1024], replicated, may hold values from 0.25 to 1.75
- qkv_coarse: bfloat16 [1024, 3072], replicated, may hold values from -0.1875 to 0.1875
- scale_coarse: float32 [16], replicated, may hold values from 2 to 24
- out_coarse: bfloat16 [1024, 1024], replicated, may hold values from -0.1875 to 0.1875
Outputs:
- fine_out: bfloat16 [256, 256, 256], P('ha', 'wa')
- coarse_out: bfloat16 [16, 16, 1024], P('ha', 'wa')
All inputs are finite; a program needn't handle non-finite values.
Results may differ from a plain program's by a relative error of at most 0.03.
Values may be sent and summed in bfloat16 or wider, within the bound.
A program may use at most 128 MiB of HBM per device.

v0:
```python
import jax
import jax.numpy as jnp
from jax import lax
from jax.sharding import PartitionSpec as P

CC = 1024
HD = 64
FFH = 768
RADIUS = 3
POOL = 16


def with_halo(cells, sides, width):
    for axis, dim in sides:
        count = lax.axis_size(axis)
        ends = count - 1
        head = lax.slice_in_dim(cells, 0, width, axis=dim)
        tail = lax.slice_in_dim(cells, cells.shape[dim] - width, cells.shape[dim], axis=dim)
        cells = jnp.concatenate(
            [
                lax.ppermute(tail, axis, [(i, (i + 1) % count) for i in range(ends)]),
                cells,
                lax.ppermute(head, axis, [((i + 1) % count, i) for i in range(ends)]),
            ],
            axis=dim,
        )
    return cells


def rms_scale(values, gain):
    values = values.astype(jnp.float32)
    return values * lax.rsqrt(jnp.mean(values * values, -1, keepdims=True) + 1e-06) * gain


def head_norm(values, heads):
    shaped = values.reshape(values.shape[:-1] + (heads, HD))
    return shaped * lax.rsqrt(jnp.mean(shaped * shaped, -1, keepdims=True) + 1e-06)


def attend_all(queries, keys_all, values_all, scales):
    cscores = (
        jnp.einsum("qhd,khd->hqk", queries, keys_all, preferred_element_type=jnp.float32)
        * (scales / HD)[:, None, None]
    )
    ctop = jnp.max(cscores, -1, keepdims=True)
    cexp = jnp.exp(cscores - ctop)
    cweights = (cexp / jnp.sum(cexp, -1, keepdims=True)).astype(jnp.bfloat16)
    return jnp.einsum(
        "hqk,khd->qhd", cweights, values_all, preferred_element_type=jnp.float32
    ).astype(jnp.bfloat16)


def shards(
    tokens,
    gain_attn,
    qkv_fine,
    scale_fine,
    out_fine,
    gain_ffn,
    ffn_in,
    ffn_out,
    up_proj,
    gain_coarse,
    qkv_coarse,
    scale_coarse,
    out_coarse,
):
    rows, cols, width = tokens.shape
    heads = width // HD
    count = rows * cols
    normed = rms_scale(tokens, gain_attn).astype(jnp.bfloat16).reshape(count, width)
    proj = jnp.dot(normed, qkv_fine, preferred_element_type=jnp.float32).reshape(
        rows, cols, 3 * width
    )
    query = head_norm(proj[..., :width], heads).astype(jnp.bfloat16).reshape(count, heads, HD)
    key_flat = head_norm(proj[..., width : 2 * width], heads).reshape(rows, cols, width)
    pairs = jnp.concatenate([key_flat, proj[..., 2 * width :]], -1).astype(jnp.bfloat16)
    padded = with_halo(pairs, (("ha", 0), ("wa", 1)), RADIUS)
    row_ids = lax.axis_index("ha") * rows + jnp.arange(rows + 2 * RADIUS, dtype=jnp.int32) - RADIUS
    col_ids = lax.axis_index("wa") * cols + jnp.arange(cols + 2 * RADIUS, dtype=jnp.int32) - RADIUS
    row_ok = (row_ids >= 0) & (row_ids < rows * lax.axis_size("ha"))
    col_ok = (col_ids >= 0) & (col_ids < cols * lax.axis_size("wa"))
    valid = row_ok[:, None] & col_ok[None, :]
    span = 2 * RADIUS + 1
    key_list = []
    value_list = []
    valid_list = []
    for shift_a in range(span):
        for shift_b in range(span):
            window = padded[shift_a : shift_a + rows, shift_b : shift_b + cols]
            key_list.append(window[..., :width])
            value_list.append(window[..., width:])
            valid_list.append(valid[shift_a : shift_a + rows, shift_b : shift_b + cols])
    key_stack = jnp.stack(key_list).reshape(span * span, count, heads, HD)
    value_stack = jnp.stack(value_list).reshape(span * span, count, heads, HD)
    valid_stack = jnp.stack(valid_list).reshape(span * span, count)
    raw = (
        jnp.einsum("nhd,snhd->hsn", query, key_stack, preferred_element_type=jnp.float32)
        * (scale_fine / HD)[:, None, None]
    )
    scores = jnp.where(valid_stack[None], raw, -1e30)
    top = jnp.max(scores, 1, keepdims=True)
    expo = jnp.exp(scores - top)
    weights = (expo / jnp.sum(expo, 1, keepdims=True)).astype(jnp.bfloat16)
    attn = jnp.einsum("hsn,snhd->nhd", weights, value_stack, preferred_element_type=jnp.float32)
    attn = attn.astype(jnp.bfloat16).reshape(count, width)
    h1 = (
        tokens.reshape(count, width).astype(jnp.float32)
        + jnp.dot(attn, out_fine, preferred_element_type=jnp.float32)
    ).astype(jnp.bfloat16)
    n2 = rms_scale(h1, gain_ffn).astype(jnp.bfloat16)
    mixed = jnp.dot(n2, ffn_in, preferred_element_type=jnp.float32)
    gated = (jax.nn.gelu(mixed[:, :FFH], approximate=True) * mixed[:, FFH:]).astype(jnp.bfloat16)
    fine_out = (
        h1.astype(jnp.float32) + jnp.dot(gated, ffn_out, preferred_element_type=jnp.float32)
    ).astype(jnp.bfloat16)
    fine_out = fine_out.reshape(rows, cols, width)
    rows_c, cols_c = (rows // POOL, cols // POOL)
    pooled = (
        fine_out.astype(jnp.float32).reshape(rows_c, POOL, cols_c, POOL, width).mean(axis=(1, 3))
    )
    pooled = pooled.astype(jnp.bfloat16).reshape(rows_c * cols_c, width)
    heads_c = CC // HD
    coarse = jnp.dot(pooled, up_proj, preferred_element_type=jnp.float32).astype(jnp.bfloat16)
    ncoarse = rms_scale(coarse, gain_coarse).astype(jnp.bfloat16)
    pc = jnp.dot(ncoarse, qkv_coarse, preferred_element_type=jnp.float32)
    cq = head_norm(pc[:, :CC], heads_c).astype(jnp.bfloat16)
    local_kv = jnp.concatenate(
        [head_norm(pc[:, CC : 2 * CC], heads_c).reshape(-1, CC), pc[:, 2 * CC :]], -1
    ).astype(jnp.bfloat16)
    all_kv = lax.all_gather(local_kv, ("ha", "wa"), axis=0, tiled=True)
    ck = all_kv[:, :CC].reshape(-1, heads_c, HD)
    cv = all_kv[:, CC:].reshape(-1, heads_c, HD)
    cattn = attend_all(cq, ck, cv, scale_coarse).reshape(-1, CC)
    coarse_out = (
        coarse.astype(jnp.float32) + jnp.dot(cattn, out_coarse, preferred_element_type=jnp.float32)
    ).astype(jnp.bfloat16)
    return (fine_out, coarse_out.reshape(rows_c, cols_c, CC))


def solution(mesh):
    return jax.shard_map(
        shards,
        mesh=mesh,
        in_specs=(P("ha", "wa", None), P(), P(), P(), P(), P(), P(), P(), P(), P(), P(), P(), P()),
        out_specs=(P("ha", "wa", None), P("ha", "wa", None)),
        check_vma=False,
    )
```

profile of v0, /device:TPU:99, one launch (start us, length us, event | category | flops | bytes accessed | tf_op | source)
XLA Modules:
  0.0 1168.6 jit_solution(1315303001375330019)
XLA Ops:
  13.5 2.1 mul.205
  17.9 2.6 collective-permute-start.1
  20.5 4.7 collective-permute-start
  68.9 2.5 collective-permute-start.3
  71.4 3.3 collective-permute-start.2
  76.5 1.8 stack.503
  100.1 1.8 stack.501
  101.9 1.8 stack.502
  103.7 1.8 stack.504
  107.2 1.8 stack.506
  112.6 1.8 stack.509
  114.4 1.8 stack.511
  118.0 1.8 stack.513
  119.8 1.8 stack.514
  121.6 1.8 stack.515
  123.4 1.8 stack.516
  132.2 1.8 stack.522
  134.0 1.8 stack.523
  137.6 1.8 stack.526
  139.4 1.8 stack.527
  141.2 1.8 stack.528
  144.8 1.8 stack.530
  146.6 1.8 stack.532
  148.4 1.8 stack.533
  155.5 1.8 stack.537
  159.1 1.8 stack.540
  162.7 1.8 stack.542
  168.0 1.8 stack.546
  171.6 1.8 stack.548
  173.6 1.9 constant_dynamic-update-slice_fusion.47
  189.5 1.9 constant_dynamic-update-slice_fusion.38
  234.9 23.5 %fusion = f32[4,256,1,49]{3,2,1,0:T(1,128)} fusion(bf16[49,256,4,64]{3,2,1,0:T(4,128)(2,1)} %constant_dynamic-update-slice_fusion, bf16[256,4,64,1]{2,1,0,3:T(4,128)(2,1)S(1)} %copy-done.48), kind=kOutput, calls=%fused_computation.1 | convolution fusion | flops 6422528 | bytes 6754304 | tf_op jit(solution)/shard_map/nhd,snhd->hsn/dot_general | solution.py:98
  260.9 5.2 copy.36
  266.1 1.8 stack.550
  271.5 1.8 stack.552
  273.3 1.8 stack.554
  278.6 1.8 stack.557
  282.2 1.8 stack.559
  284.0 1.8 stack.561
  285.8 1.8 stack.562
  287.6 1.8 stack.563
  296.5 1.8 stack.569
  298.3 1.8 stack.570
  300.1 1.8 stack.571
  305.5 1.8 stack.575
  307.3 1.8 stack.576
  309.1 1.8 stack.577
  310.9 1.8 stack.578
  312.7 1.8 stack.579
  314.5 1.8 stack.580
  316.3 1.8 stack.582
  318.1 1.8 stack.583
  319.9 1.8 stack.584
  323.4 1.8 stack.586
  334.1 1.8 stack.593
  336.8 1.8 stack.596
  338.6 1.8 stack.597
  340.4 1.8 stack.598
  342.3 1.9 constant_dynamic-update-slice_fusion.96
  402.8 18.4 %multiply_reduce_fusion = bf16[256,4,64]{2,1,0:T(4,128)(2,1)S(1)} fusion(f32[256,4,49]{1,0,2:T(8,128)} %copy.36, bf16[49,256,4,64]{3,2,1,0:T(4,128)(2,1)} %constant_dynamic-update-slice_fusion.49), kind=kLoop, calls=%fused_computation | loop fusion | flops 9568256 | bytes 6754304
  423.3 2.1 convert_reduce_fusion
  426.9 3.7 fusion.60
  432.0 722.7 %all-gather.3.cloned.1.call-done = bf16[256,1,2048]{2,1,0:T(2,128)(2,1)} async-done(((bf16[1,1,2048]{2,1,0:T(2,128)(2,1)}), bf16[256,1,2048]{2,1,0:T(2,128)(2,1)}) %all-gather.3.cloned.1.call-update) | async-done | bytes 1048592 | tf_op jit(solution)/shard_map/all_gather | solution.py:131
  1154.7 2.2 copy.55
  (381 shorter events, 265.8 us)
Async XLA Ops:
  7.2 1153.1 %copy-start = (bf16[1024,1024]{1,0:T(8,128)(2,1)S(1)}, bf16[1024,1024]{1,0:T(8,128)(2,1)}, u32[]{:S(2)}) copy-start(bf16[1024,1024]{1,0:T(8,128)(2,1)} %param.25) | copy-start | bytes 6291460
  7.2 1147.6 %all-gather.3.cloned.1.call-start = ((), (), s32[]{:S(2)}) async-start(), calls=%async_computation | async-start | bytes 2105344 | tf_op jit(solution)/shard_map/all_gather | solution.py:131
  17.9 49.4 %collective-permute-start.1 = (bf16[3,16,512]{2,1,0:T(8,128)(2,1)}, bf16[3,16,512]{2,1,0:T(8,128)(2,1)}, u32[]{:S(2)}, u32[]{:S(2)}) collective-permute-start(bf16[3,16,512]{2,1,0:T(8,128)(2,1)} %get-tuple-element.113), channel_id=1, source_target_pairs={{16,0},{32,16},{48,32},{64,48},{80,64},{96,80},{112,96},{128,112},... | collective-permute-start | bytes 147464 | tf_op jit(solution)/shard_map/ppermute | solution.py:23
  20.5 46.9 %collective-permute-start = (bf16[3,16,512]{2,1,0:T(8,128)(2,1)}, bf16[3,16,512]{2,1,0:T(8,128)(2,1)}, u32[]{:S(2)}, u32[]{:S(2)}) collective-permute-start(bf16[3,16,512]{2,1,0:T(8,128)(2,1)} %get-tuple-element.112), channel_id=1, source_target_pairs={{0,16},{16,32},{32,48},{48,64},{64,80},{80,96},{96,112},{112,128},... | collective-permute-start | bytes 147464 | tf_op jit(solution)/shard_map/ppermute | solution.py:21
  68.9 20.5 %collective-permute-start.3 = (bf16[22,3,512]{2,1,0:T(4,128)(2,1)}, bf16[22,3,512]{2,1,0:T(4,128)(2,1)}, u32[]{:S(2)}, u32[]{:S(2)}) collective-permute-start(bf16[22,3,512]{2,1,0:T(4,128)(2,1)} %get-tuple-element.96), channel_id=1, source_target_pairs={{1,0},{2,1},{3,2},{4,3},{5,4},{6,5},{7,6},{8,7},{9,8},{10,9},{11,1... | collective-permute-start | bytes 202760 | tf_op jit(solution)/shard_map/ppermute | solution.py:23
  71.4 18.0 %collective-permute-start.2 = (bf16[22,3,512]{2,1,0:T(4,128)(2,1)}, bf16[22,3,512]{2,1,0:T(4,128)(2,1)}, u32[]{:S(2)}, u32[]{:S(2)}) collective-permute-start(bf16[22,3,512]{2,1,0:T(4,128)(2,1)} %get-tuple-element.97), channel_id=1, source_target_pairs={{0,1},{1,2},{2,3},{3,4},{4,5},{5,6},{6,7},{7,8},{8,9},{9,10},{10,1... | collective-permute-start | bytes 202760 | tf_op jit(solution)/shard_map/ppermute | solution.py:21
  112.6 101.5 %copy-start.3 = (bf16[1,256,4,64]{3,2,1,0:T(4,128)(2,1)S(1)}, bf16[1,256,4,64]{3,2,1,0:T(4,128)(2,1)}, u32[]{:S(2)}) copy-start(bf16[1,256,4,64]{3,2,1,0:T(4,128)(2,1)} %stack.524) | copy-start | bytes 393220
  173.4 43.2 %copy-start.46 = (bf16[1,256,4,64]{3,2,1,0:T(4,128)(2,1)S(1)}, bf16[1,256,4,64]{3,2,1,0:T(4,128)(2,1)}, u32[]{:S(2)}) copy-start(bf16[1,256,4,64]{3,2,1,0:T(4,128)(2,1)} %stack.526) | copy-start | bytes 393220
  173.4 44.0 %copy-start.45 = (bf16[1,256,4,64]{3,2,1,0:T(4,128)(2,1)S(1)}, bf16[1,256,4,64]{3,2,1,0:T(4,128)(2,1)}, u32[]{:S(2)}) copy-start(bf16[1,256,4,64]{3,2,1,0:T(4,128)(2,1)} %stack.527) | copy-start | bytes 393220
  173.4 44.8 %copy-start.43 = (bf16[1,256,4,64]{3,2,1,0:T(4,128)(2,1)S(1)}, bf16[1,256,4,64]{3,2,1,0:T(4,128)(2,1)}, u32[]{:S(2)}) copy-start(bf16[1,256,4,64]{3,2,1,0:T(4,128)(2,1)} %stack.528) | copy-start | bytes 393220
  173.4 45.6 %copy-start.41 = (bf16[1,256,4,64]{3,2,1,0:T(4,128)(2,1)S(1)}, bf16[1,256,4,64]{3,2,1,0:T(4,128)(2,1)}, u32[]{:S(2)}) copy-start(bf16[1,256,4,64]{3,2,1,0:T(4,128)(2,1)} %stack.529) | copy-start | bytes 393220
  173.4 46.4 %copy-start.39 = (bf16[1,256,4,64]{3,2,1,0:T(4,128)(2,1)S(1)}, bf16[1,256,4,64]{3,2,1,0:T(4,128)(2,1)}, u32[]{:S(2)}) copy-start(bf16[1,256,4,64]{3,2,1,0:T(4,128)(2,1)} %stack.530) | copy-start | bytes 393220
  173.4 47.2 %copy-start.6 = (bf16[1,256,4,64]{3,2,1,0:T(4,128)(2,1)S(1)}, bf16[1,256,4,64]{3,2,1,0:T(4,128)(2,1)}, u32[]{:S(2)}) copy-start(bf16[1,256,4,64]{3,2,1,0:T(4,128)(2,1)} %stack.531) | copy-start | bytes 393220
  173.4 48.0 %copy-start.36 = (bf16[1,256,4,64]{3,2,1,0:T(4,128)(2,1)S(1)}, bf16[1,256,4,64]{3,2,1,0:T(4,128)(2,1)}, u32[]{:S(2)}) copy-start(bf16[1,256,4,64]{3,2,1,0:T(4,128)(2,1)} %stack.532) | copy-start | bytes 393220
  173.4 48.7 %copy-start.35 = (bf16[1,256,4,64]{3,2,1,0:T(4,128)(2,1)S(1)}, bf16[1,256,4,64]{3,2,1,0:T(4,128)(2,1)}, u32[]{:S(2)}) copy-start(bf16[1,256,4,64]{3,2,1,0:T(4,128)(2,1)} %stack.533) | copy-start | bytes 393220
  173.5 49.5 %copy-start.33 = (bf16[1,256,4,64]{3,2,1,0:T(4,128)(2,1)S(1)}, bf16[1,256,4,64]{3,2,1,0:T(4,128)(2,1)}, u32[]{:S(2)}) copy-start(bf16[1,256,4,64]{3,2,1,0:T(4,128)(2,1)} %stack.534) | copy-start | bytes 393220
  173.5 50.3 %copy-start.31 = (bf16[1,256,4,64]{3,2,1,0:T(4,128)(2,1)S(1)}, bf16[1,256,4,64]{3,2,1,0:T(4,128)(2,1)}, u32[]{:S(2)}) copy-start(bf16[1,256,4,64]{3,2,1,0:T(4,128)(2,1)} %stack.535) | copy-start | bytes 393220
  173.5 51.1 %copy-start.29 = (bf16[1,256,4,64]{3,2,1,0:T(4,128)(2,1)S(1)}, bf16[1,256,4,64]{3,2,1,0:T(4,128)(2,1)}, u32[]{:S(2)}) copy-start(bf16[1,256,4,64]{3,2,1,0:T(4,128)(2,1)} %stack.536) | copy-start | bytes 393220
  173.5 51.9 %copy-start.27 = (bf16[1,256,4,64]{3,2,1,0:T(4,128)(2,1)S(1)}, bf16[1,256,4,64]{3,2,1,0:T(4,128)(2,1)}, u32[]{:S(2)}) copy-start(bf16[1,256,4,64]{3,2,1,0:T(4,128)(2,1)} %stack.537) | copy-start | bytes 393220
  173.5 52.7 %copy-start.5 = (bf16[1,256,4,64]{3,2,1,0:T(4,128)(2,1)S(1)}, bf16[1,256,4,64]{3,2,1,0:T(4,128)(2,1)}, u32[]{:S(2)}) copy-start(bf16[1,256,4,64]{3,2,1,0:T(4,128)(2,1)} %stack.538) | copy-start | bytes 393220
  173.5 53.5 %copy-start.24 = (bf16[1,256,4,64]{3,2,1,0:T(4,128)(2,1)S(1)}, bf16[1,256,4,64]{3,2,1,0:T(4,128)(2,1)}, u32[]{:S(2)}) copy-start(bf16[1,256,4,64]{3,2,1,0:T(4,128)(2,1)} %stack.539) | copy-start | bytes 393220
  173.5 54.3 %copy-start.23 = (bf16[1,256,4,64]{3,2,1,0:T(4,128)(2,1)S(1)}, bf16[1,256,4,64]{3,2,1,0:T(4,128)(2,1)}, u32[]{:S(2)}) copy-start(bf16[1,256,4,64]{3,2,1,0:T(4,128)(2,1)} %stack.540) | copy-start | bytes 393220
  173.5 55.0 %copy-start.21 = (bf16[1,256,4,64]{3,2,1,0:T(4,128)(2,1)S(1)}, bf16[1,256,4,64]{3,2,1,0:T(4,128)(2,1)}, u32[]{:S(2)}) copy-start(bf16[1,256,4,64]{3,2,1,0:T(4,128)(2,1)} %stack.541) | copy-start | bytes 393220
  173.5 55.8 %copy-start.19 = (bf16[1,256,4,64]{3,2,1,0:T(4,128)(2,1)S(1)}, bf16[1,256,4,64]{3,2,1,0:T(4,128)(2,1)}, u32[]{:S(2)}) copy-start(bf16[1,256,4,64]{3,2,1,0:T(4,128)(2,1)} %stack.542) | copy-start | bytes 393220
  173.5 56.6 %copy-start.17 = (bf16[1,256,4,64]{3,2,1,0:T(4,128)(2,1)S(1)}, bf16[1,256,4,64]{3,2,1,0:T(4,128)(2,1)}, u32[]{:S(2)}) copy-start(bf16[1,256,4,64]{3,2,1,0:T(4,128)(2,1)} %stack.543) | copy-start | bytes 393220
  173.6 57.4 %copy-start.15 = (bf16[1,256,4,64]{3,2,1,0:T(4,128)(2,1)S(1)}, bf16[1,256,4,64]{3,2,1,0:T(4,128)(2,1)}, u32[]{:S(2)}) copy-start(bf16[1,256,4,64]{3,2,1,0:T(4,128)(2,1)} %stack.544) | copy-start | bytes 393220
  173.6 58.2 %copy-start.4 = (bf16[1,256,4,64]{3,2,1,0:T(4,128)(2,1)S(1)}, bf16[1,256,4,64]{3,2,1,0:T(4,128)(2,1)}, u32[]{:S(2)}) copy-start(bf16[1,256,4,64]{3,2,1,0:T(4,128)(2,1)} %stack.545) | copy-start | bytes 393220
  173.6 59.0 %copy-start.12 = (bf16[1,256,4,64]{3,2,1,0:T(4,128)(2,1)S(1)}, bf16[1,256,4,64]{3,2,1,0:T(4,128)(2,1)}, u32[]{:S(2)}) copy-start(bf16[1,256,4,64]{3,2,1,0:T(4,128)(2,1)} %stack.546) | copy-start | bytes 393220
  173.6 59.8 %copy-start.10 = (bf16[1,256,4,64]{3,2,1,0:T(4,128)(2,1)S(1)}, bf16[1,256,4,64]{3,2,1,0:T(4,128)(2,1)}, u32[]{:S(2)}) copy-start(bf16[1,256,4,64]{3,2,1,0:T(4,128)(2,1)} %stack.547) | copy-start | bytes 393220
  173.6 60.5 %copy-start.7 = (bf16[1,256,4,64]{3,2,1,0:T(4,128)(2,1)S(1)}, bf16[1,256,4,64]{3,2,1,0:T(4,128)(2,1)}, u32[]{:S(2)}) copy-start(bf16[1,256,4,64]{3,2,1,0:T(4,128)(2,1)} %stack.548) | copy-start | bytes 393220
  173.6 61.3 %copy-start.48 = (bf16[256,4,64,1]{2,1,0,3:T(4,128)(2,1)S(1)}, bf16[256,4,64,1]{2,1,0,3:T(4,128)(2,1)}, u32[]{:S(2)}) copy-start(bf16[256,4,64,1]{2,1,0,3:T(4,128)(2,1)} %fusion.22) | copy-start | bytes 393220
  231.7 28.0 %copy-start.50 = (f32[4]{0:T(128)S(1)}, f32[4]{0:T(128)}, u32[]{:S(2)}) copy-start(f32[4]{0:T(128)} %broadcast_multiply_fusion.1) | copy-start | bytes 52
  266.1 104.3 %copy-start.2 = (bf16[1,256,4,64]{3,2,1,0:T(4,128)(2,1)S(1)}, bf16[1,256,4,64]{3,2,1,0:T(4,128)(2,1)}, u32[]{:S(2)}) copy-start(bf16[1,256,4,64]{3,2,1,0:T(4,128)(2,1)} %stack.567) | copy-start | bytes 393220
  342.2 42.1 %copy-start.44 = (bf16[1,256,4,64]{3,2,1,0:T(4,128)(2,1)S(1)}, bf16[1,256,4,64]{3,2,1,0:T(4,128)(2,1)}, u32[]{:S(2)}) copy-start(bf16[1,256,4,64]{3,2,1,0:T(4,128)(2,1)} %stack.576) | copy-start | bytes 393220
  342.2 42.9 %copy-start.42 = (bf16[1,256,4,64]{3,2,1,0:T(4,128)(2,1)S(1)}, bf16[1,256,4,64]{3,2,1,0:T(4,128)(2,1)}, u32[]{:S(2)}) copy-start(bf16[1,256,4,64]{3,2,1,0:T(4,128)(2,1)} %stack.577) | copy-start | bytes 393220
  342.2 43.7 %copy-start.40 = (bf16[1,256,4,64]{3,2,1,0:T(4,128)(2,1)S(1)}, bf16[1,256,4,64]{3,2,1,0:T(4,128)(2,1)}, u32[]{:S(2)}) copy-start(bf16[1,256,4,64]{3,2,1,0:T(4,128)(2,1)} %stack.578) | copy-start | bytes 393220
  342.2 44.5 %copy-start.38 = (bf16[1,256,4,64]{3,2,1,0:T(4,128)(2,1)S(1)}, bf16[1,256,4,64]{3,2,1,0:T(4,128)(2,1)}, u32[]{:S(2)}) copy-start(bf16[1,256,4,64]{3,2,1,0:T(4,128)(2,1)} %stack.579) | copy-start | bytes 393220
  342.2 45.3 %copy-start.37 = (bf16[1,256,4,64]{3,2,1,0:T(4,128)(2,1)S(1)}, bf16[1,256,4,64]{3,2,1,0:T(4,128)(2,1)}, u32[]{:S(2)}) copy-start(bf16[1,256,4,64]{3,2,1,0:T(4,128)(2,1)} %stack.580) | copy-start | bytes 393220
  342.2 46.9 %copy-start.34 = (bf16[1,256,4,64]{3,2,1,0:T(4,128)(2,1)S(1)}, bf16[1,256,4,64]{3,2,1,0:T(4,128)(2,1)}, u32[]{:S(2)}) copy-start(bf16[1,256,4,64]{3,2,1,0:T(4,128)(2,1)} %stack.582) | copy-start | bytes 393220
  342.2 47.7 %copy-start.32 = (bf16[1,256,4,64]{3,2,1,0:T(4,128)(2,1)S(1)}, bf16[1,256,4,64]{3,2,1,0:T(4,128)(2,1)}, u32[]{:S(2)}) copy-start(bf16[1,256,4,64]{3,2,1,0:T(4,128)(2,1)} %stack.583) | copy-start | bytes 393220
  342.2 48.5 %copy-start.30 = (bf16[1,256,4,64]{3,2,1,0:T(4,128)(2,1)S(1)}, bf16[1,256,4,64]{3,2,1,0:T(4,128)(2,1)}, u32[]{:S(2)}) copy-start(bf16[1,256,4,64]{3,2,1,0:T(4,128)(2,1)} %stack.584) | copy-start | bytes 393220
  342.2 49.3 %copy-start.28 = (bf16[1,256,4,64]{3,2,1,0:T(4,128)(2,1)S(1)}, bf16[1,256,4,64]{3,2,1,0:T(4,128)(2,1)}, u32[]{:S(2)}) copy-start(bf16[1,256,4,64]{3,2,1,0:T(4,128)(2,1)} %stack.585) | copy-start | bytes 393220
  342.2 50.1 %copy-start.26 = (bf16[1,256,4,64]{3,2,1,0:T(4,128)(2,1)S(1)}, bf16[1,256,4,64]{3,2,1,0:T(4,128)(2,1)}, u32[]{:S(2)}) copy-start(bf16[1,256,4,64]{3,2,1,0:T(4,128)(2,1)} %stack.586) | copy-start | bytes 393220
  342.2 50.9 %copy-start.25 = (bf16[1,256,4,64]{3,2,1,0:T(4,128)(2,1)S(1)}, bf16[1,256,4,64]{3,2,1,0:T(4,128)(2,1)}, u32[]{:S(2)}) copy-start(bf16[1,256,4,64]{3,2,1,0:T(4,128)(2,1)} %stack.587) | copy-start | bytes 393220
  342.2 52.5 %copy-start.22 = (bf16[1,256,4,64]{3,2,1,0:T(4,128)(2,1)S(1)}, bf16[1,256,4,64]{3,2,1,0:T(4,128)(2,1)}, u32[]{:S(2)}) copy-start(bf16[1,256,4,64]{3,2,1,0:T(4,128)(2,1)} %stack.589) | copy-start | bytes 393220
  342.3 53.3 %copy-start.20 = (bf16[1,256,4,64]{3,2,1,0:T(4,128)(2,1)S(1)}, bf16[1,256,4,64]{3,2,1,0:T(4,128)(2,1)}, u32[]{:S(2)}) copy-start(bf16[1,256,4,64]{3,2,1,0:T(4,128)(2,1)} %stack.590) | copy-start | bytes 393220
  342.3 54.1 %copy-start.18 = (bf16[1,256,4,64]{3,2,1,0:T(4,128)(2,1)S(1)}, bf16[1,256,4,64]{3,2,1,0:T(4,128)(2,1)}, u32[]{:S(2)}) copy-start(bf16[1,256,4,64]{3,2,1,0:T(4,128)(2,1)} %stack.591) | copy-start | bytes 393220
  342.3 54.9 %copy-start.16 = (bf16[1,256,4,64]{3,2,1,0:T(4,128)(2,1)S(1)}, bf16[1,256,4,64]{3,2,1,0:T(4,128)(2,1)}, u32[]{:S(2)}) copy-start(bf16[1,256,4,64]{3,2,1,0:T(4,128)(2,1)} %stack.592) | copy-start | bytes 393220
  342.3 55.7 %copy-start.13 = (bf16[1,256,4,64]{3,2,1,0:T(4,128)(2,1)S(1)}, bf16[1,256,4,64]{3,2,1,0:T(4,128)(2,1)}, u32[]{:S(2)}) copy-start(bf16[1,256,4,64]{3,2,1,0:T(4,128)(2,1)} %stack.593) | copy-start | bytes 393220
  342.3 56.5 %copy-start.14 = (bf16[1,256,4,64]{3,2,1,0:T(4,128)(2,1)S(1)}, bf16[1,256,4,64]{3,2,1,0:T(4,128)(2,1)}, u32[]{:S(2)}) copy-start(bf16[1,256,4,64]{3,2,1,0:T(4,128)(2,1)} %stack.594) | copy-start | bytes 393220
  342.3 58.1 %copy-start.11 = (bf16[1,256,4,64]{3,2,1,0:T(4,128)(2,1)S(1)}, bf16[1,256,4,64]{3,2,1,0:T(4,128)(2,1)}, u32[]{:S(2)}) copy-start(bf16[1,256,4,64]{3,2,1,0:T(4,128)(2,1)} %stack.596) | copy-start | bytes 393220
  342.3 58.9 %copy-start.8 = (bf16[1,256,4,64]{3,2,1,0:T(4,128)(2,1)S(1)}, bf16[1,256,4,64]{3,2,1,0:T(4,128)(2,1)}, u32[]{:S(2)}) copy-start(bf16[1,256,4,64]{3,2,1,0:T(4,128)(2,1)} %stack.597) | copy-start | bytes 393220
  342.3 59.7 %copy-start.9 = (bf16[1,256,4,64]{3,2,1,0:T(4,128)(2,1)S(1)}, bf16[1,256,4,64]{3,2,1,0:T(4,128)(2,1)}, u32[]{:S(2)}) copy-start(bf16[1,256,4,64]{3,2,1,0:T(4,128)(2,1)} %stack.598) | copy-start | bytes 393220
  394.0 27.4 %copy-start.1 = (bf16[16,16,256]{2,1,0:T(8,128)(2,1)S(1)}, bf16[16,16,256]{2,1,0:T(8,128)(2,1)}, u32[]{:S(2)}) copy-start(bf16[16,16,256]{2,1,0:T(8,128)(2,1)} %param.13) | copy-start | bytes 393220
  394.0 27.4 %copy-start.49 = (bf16[256,256]{1,0:T(8,128)(2,1)S(1)}, bf16[256,256]{1,0:T(8,128)(2,1)}, u32[]{:S(2)}) copy-start(bf16[256,256]{1,0:T(8,128)(2,1)} %param.17) | copy-start | bytes 393220
  394.8 27.0 %copy-start.52 = (f32[256]{0:T(256)S(1)}, f32[256]{0:T(256)}, u32[]{:S(2)}) copy-start(f32[256]{0:T(256)} %param.18) | copy-start | bytes 3076
  402.8 22.6 %copy-start.47 = (bf16[256,1024]{1,0:T(8,128)(2,1)S(1)}, bf16[256,1024]{1,0:T(8,128)(2,1)}, u32[]{:S(2)}) copy-start(bf16[256,1024]{1,0:T(8,128)(2,1)} %param.21) | copy-start | bytes 1572868
  402.8 24.1 %copy-start.51 = (f32[1024]{0:T(1024)S(1)}, f32[1024]{0:T(1024)}, u32[]{:S(2)}) copy-start(f32[1024]{0:T(1024)} %param.22) | copy-start | bytes 12292
  402.8 28.9 %copy-start.53 = (f32[16]{0:T(128)S(1)}, f32[16]{0:T(128)}, u32[]{:S(2)}) copy-start(f32[16]{0:T(128)} %param.24) | copy-start | bytes 196
Sparse Core Ops, SparseCore 0:
  431.8 722.9 all-gather.2
where the time goes:
time: 1180 us; the launch traced here: 1170 us
  waiting for transfers between devices  723 us (61%)
  local copies, waits for them, and re-layouts  349 us (30%)
  matrix products  34.6 us (3%)
  other arithmetic  33.1 us (3%)
  between operations  16 us (1%)
  starting transfers between devices  13.1 us (1%)
    all_gather x1, waiting for transfers between devices, shards(): all_kv = lax.all_gather(local_kv, ('ha', 'wa'), axis=0, tiled=True)  723 us
    unnamed x206, local copies, waits for them, and re-layouts  130 us
    another operation x50, local copies, waits for them, and re-layouts, shards(): key_stack = jnp.stack(key_list).reshape(span * span, count, heads, HD)  85.8 us
    another operation x50, local copies, waits for them, and re-layouts, shards(): value_stack = jnp.stack(value_list).reshape(span * span, count, heads, HD)  78.3 us
    another operation x50, local copies, waits for them, and re-layouts, shards(): valid_stack = jnp.stack(valid_list).reshape(span * span, count)  34.8 us
  transfers between devices with their start and end apart: 5, of which 1 were waited for; matrix products, arithmetic and copies ran while one was open for 5% of the time, Pallas kernels for 0%

commit v1 on v0

--- a/solution.py
+++ b/solution.py
@@ -128,7 +128,10 @@
     local_kv = jnp.concatenate(
         [head_norm(pc[:, CC : 2 * CC], heads_c).reshape(-1, CC), pc[:, 2 * CC :]], -1
     ).astype(jnp.bfloat16)
-    all_kv = lax.all_gather(local_kv, ("ha", "wa"), axis=0, tiled=True)
+    peers = lax.axis_size(("ha", "wa"))
+    tiles = jnp.stack([local_kv for _ in range(peers)])
+    tiles = lax.all_to_all(tiles, ("ha", "wa"), split_axis=0, concat_axis=0)
+    all_kv = jnp.concatenate(tiles, axis=0)
     ck = all_kv[:, :CC].reshape(-1, heads_c, HD)
     cv = all_kv[:, CC:].reshape(-1, heads_c, HD)
     cattn = attend_all(cq, ck, cv, scale_coarse).reshape(-1, CC)

time: 1180 us -> 504 us (0.43)
  the two profiles are of different devices: /device:TPU:99 before, /device:TPU:1 now
where the time goes in v1:
time: 504 us; the launch traced here: 496 us
  local copies, waits for them, and re-layouts  357 us (71%)
  other arithmetic  40.6 us (8%)
  matrix products  34.6 us (7%)
  waiting for transfers between devices  31.4 us (6%)
  starting transfers between devices  29.2 us (6%)
    unnamed x208, local copies, waits for them, and re-layouts  136 us
    another operation x50, local copies, waits for them, and re-layouts, shards(): key_stack = jnp.stack(key_list).reshape(span * span, count, heads, HD)  86.1 us
    another operation x50, local copies, waits for them, and re-layouts, shards(): value_stack = jnp.stack(value_list).reshape(span * span, count, heads, HD)  78.2 us
    another operation x50, local copies, waits for them, and re-layouts, shards(): valid_stack = jnp.stack(valid_list).reshape(span * span, count)  34.7 us
    all_to_all x1, waiting for transfers between devices, shards(): tiles = lax.all_to_all(tiles, ('ha', 'wa'), split_axis=0, concat_axis=0)  31.3 us
    dot_general x1, matrix products, shards(): jnp.einsum('nhd,snhd->hsn', query, key_stack, preferred_element_type=jnp....  23.5 us
    unnamed x2, other arithmetic  19.2 us
    all_to_all x1, starting transfers between devices, shards(): tiles = lax.all_to_all(tiles, ('ha', 'wa'), split_axis=0, concat_axis=0)  15 us
  transfers between devices with their start and end apart: 5, of which 1 were waited for; matrix products, arithmetic and copies ran while one was open for 12% of the time, Pallas kernels for 0%

profile of v1, /device:TPU:1, one launch (start us, length us, event | category | flops | bytes accessed | tf_op | source)
XLA Modules:
  0.0 495.6 jit_solution(15493275249697088684)
XLA Ops:
  6.9 2.1 mul.205
  11.3 5.1 %collective-permute-start.1 = (bf16[3,16,512]{2,1,0:T(8,128)(2,1)}, bf16[3,16,512]{2,1,0:T(8,128)(2,1)}, u32[]{:S(2)}, u32[]{:S(2)}) collective-permute-start(bf16[3,16,512]{2,1,0:T(8,128)(2,1)} %get-tuple-element.115), channel_id=1, source_target_pairs={{16,0},{32,16},{48,32},{64,48},{80,64},{96,80},{112,96},{128,112},... | collective-permute-start | bytes 147464 | tf_op jit(solution)/shard_map/ppermute | solution.py:23
  16.4 3.0 collective-permute-start
  64.4 4.8 collective-permute-start.2
  78.1 1.8 stack.390
  98.2 1.8 stack.356
  100.0 1.8 stack.357
  101.8 1.8 stack.358
  103.6 1.8 stack.359
  107.2 1.8 stack.361
  112.5 1.8 stack.365
  114.4 1.8 stack.366
  116.2 1.8 stack.367
  117.9 1.8 stack.368
  121.5 1.8 stack.371
  125.1 1.8 stack.373
  126.9 1.8 stack.374
  128.7 1.8 stack.375
  132.3 1.8 stack.378
  137.6 1.8 stack.381
  139.4 1.8 stack.382
  141.2 1.8 stack.384
  143.1 1.8 stack.385
  144.9 1.8 stack.386
  150.2 1.8 stack.389
  152.0 1.8 stack.391
  155.6 1.8 stack.393
  157.4 1.8 stack.394
  159.2 1.8 stack.395
  161.0 1.8 stack.396
  162.8 1.8 stack.398
  164.6 1.8 stack.399
  168.4 1.9 constant_dynamic-update-slice_fusion.47
  184.4 2.2 constant_dynamic-update-slice_fusion.38
  230.3 23.5 %fusion = f32[4,256,1,49]{3,2,1,0:T(1,128)} fusion(bf16[49,256,4,64]{3,2,1,0:T(4,128)(2,1)} %constant_dynamic-update-slice_fusion, bf16[256,4,64,1]{2,1,0,3:T(4,128)(2,1)S(1)} %copy-done.48), kind=kOutput, calls=%fused_computation.1 | convolution fusion | flops 6422528 | bytes 6754304 | tf_op jit(solution)/shard_map/nhd,snhd->hsn/dot_general | solution.py:98
  256.4 5.1 %copy.36 = f32[256,4,49]{1,0,2:T(8,128)} copy(f32[256,4,49]{0,1,2:T(4,128)} %bitcast_convert_fusion) | data formatting | bytes 401408
  261.5 1.8 stack.402
  266.9 1.8 stack.404
  270.5 1.8 stack.814
  274.1 1.8 stack.816
  275.9 1.8 stack.817
  277.6 1.8 stack.818
  279.4 1.8 stack.820
  288.4 1.8 stack.825
  293.7 1.8 stack.829
  295.5 1.8 stack.830
  299.1 1.8 stack.832
  309.8 1.8 stack.839
  311.6 1.8 stack.841
  315.2 1.8 stack.843
  317.0 1.8 stack.844
  324.1 1.8 stack.849
  325.9 1.8 stack.850
  327.7 1.8 stack.851
  337.6 1.9 constant_dynamic-update-slice_fusion.96
  398.0 18.4 %multiply_reduce_fusion = bf16[256,4,64]{2,1,0:T(4,128)(2,1)S(1)} fusion(f32[256,4,49]{1,0,2:T(8,128)} %copy.36, bf16[49,256,4,64]{3,2,1,0:T(4,128)(2,1)} %constant_dynamic-update-slice_fusion.49), kind=kLoop, calls=%fused_computation | loop fusion | flops 9568256 | bytes 6754304
  418.4 2.1 convert_reduce_fusion
  422.1 3.7 fusion.61
  426.2 2.4 stack.859
  429.2 8.0 %reduce.30 = bf16[256,2048]{1,0:T(8,128)(2,1)S(1)} reduce(bf16[256,1,2048]{2,1,0:T(2,128)(2,1)} %stack.859, bf16[]{:T(256)} %broadcast.205), dimensions={1}, to_apply=%stack.859.reduce_sub_computation | reduce | bytes 2097154 | tf_op jit(solution)/shard_map/stack | solution.py:132
  438.8 15.0 %all-to-all-start = ((bf16[256,2,1024]{2,1,0:T(2,128)(2,1)}), bf16[256,2,1024]{2,1,0:T(2,128)(2,1)S(1)}, u32[]{:S(2)}, u32[]{:S(2)}) async-start(bf16[256,2,1024]{2,1,0:T(2,128)(2,1)} %reshape.621), calls=%async_computation | async-start | bytes 2097152 | tf_op jit(solution)/shard_map/all_to_all | solution.py:133
  454.2 31.3 %all-to-all-done = bf16[256,2,1024]{2,1,0:T(2,128)(2,1)S(1)} async-done(((bf16[256,2,1024]{2,1,0:T(2,128)(2,1)}), bf16[256,2,1024]{2,1,0:T(2,128)(2,1)S(1)}, u32[]{:S(2)}, u32[]{:S(2)}) %all-to-all-start) | async-done | bytes 1048608 | tf_op jit(solution)/shard_map/all_to_all | solution.py:133
  485.5 3.3 reshape.622
  488.8 2.2 copy.55
  (384 shorter events, 274.3 us)
Async XLA Ops:
  0.6 493.7 %copy-start = (bf16[1024,1024]{1,0:T(8,128)(2,1)S(1)}, bf16[1024,1024]{1,0:T(8,128)(2,1)}, u32[]{:S(2)}) copy-start(bf16[1024,1024]{1,0:T(8,128)(2,1)} %param.25) | copy-start | bytes 6291460
  11.3 50.3 %collective-permute-start.1 = (bf16[3,16,512]{2,1,0:T(8,128)(2,1)}, bf16[3,16,512]{2,1,0:T(8,128)(2,1)}, u32[]{:S(2)}, u32[]{:S(2)}) collective-permute-start(bf16[3,16,512]{2,1,0:T(8,128)(2,1)} %get-tuple-element.115), channel_id=1, source_target_pairs={{16,0},{32,16},{48,32},{64,48},{80,64},{96,80},{112,96},{128,112},... | collective-permute-start | bytes 147464 | tf_op jit(solution)/shard_map/ppermute | solution.py:23
  16.4 45.2 %collective-permute-start = (bf16[3,16,512]{2,1,0:T(8,128)(2,1)}, bf16[3,16,512]{2,1,0:T(8,128)(2,1)}, u32[]{:S(2)}, u32[]{:S(2)}) collective-permute-start(bf16[3,16,512]{2,1,0:T(8,128)(2,1)} %get-tuple-element.114), channel_id=1, source_target_pairs={{0,16},{16,32},{32,48},{48,64},{64,80},{80,96},{96,112},{112,128},... | collective-permute-start | bytes 147464 | tf_op jit(solution)/shard_map/ppermute | solution.py:21
  63.1 20.8 %collective-permute-start.3 = (bf16[22,3,512]{2,1,0:T(4,128)(2,1)}, bf16[22,3,512]{2,1,0:T(4,128)(2,1)}, u32[]{:S(2)}, u32[]{:S(2)}) collective-permute-start(bf16[22,3,512]{2,1,0:T(4,128)(2,1)} %get-tuple-element.98), channel_id=1, source_target_pairs={{1,0},{2,1},{3,2},{4,3},{5,4},{6,5},{7,6},{8,7},{9,8},{10,9},{11,1... | collective-permute-start | bytes 202760 | tf_op jit(solution)/shard_map/ppermute | solution.py:23
  64.4 19.5 %collective-permute-start.2 = (bf16[22,3,512]{2,1,0:T(4,128)(2,1)}, bf16[22,3,512]{2,1,0:T(4,128)(2,1)}, u32[]{:S(2)}, u32[]{:S(2)}) collective-permute-start(bf16[22,3,512]{2,1,0:T(4,128)(2,1)} %get-tuple-element.99), channel_id=1, source_target_pairs={{0,1},{1,2},{2,3},{3,4},{4,5},{5,6},{6,7},{7,8},{8,9},{9,10},{10,1... | collective-permute-start | bytes 202760 | tf_op jit(solution)/shard_map/ppermute | solution.py:21
  107.2 102.1 %copy-start.3 = (bf16[1,256,4,64]{3,2,1,0:T(4,128)(2,1)S(1)}, bf16[1,256,4,64]{3,2,1,0:T(4,128)(2,1)}, u32[]{:S(2)}) copy-start(bf16[1,256,4,64]{3,2,1,0:T(4,128)(2,1)} %stack.376) | copy-start | bytes 393220
  168.2 43.6 %copy-start.46 = (bf16[1,256,4,64]{3,2,1,0:T(4,128)(2,1)S(1)}, bf16[1,256,4,64]{3,2,1,0:T(4,128)(2,1)}, u32[]{:S(2)}) copy-start(bf16[1,256,4,64]{3,2,1,0:T(4,128)(2,1)} %stack.378) | copy-start | bytes 393220
  168.2 44.4 %copy-start.45 = (bf16[1,256,4,64]{3,2,1,0:T(4,128)(2,1)S(1)}, bf16[1,256,4,64]{3,2,1,0:T(4,128)(2,1)}, u32[]{:S(2)}) copy-start(bf16[1,256,4,64]{3,2,1,0:T(4,128)(2,1)} %stack.379) | copy-start | bytes 393220
  168.2 45.3 %copy-start.43 = (bf16[1,256,4,64]{3,2,1,0:T(4,128)(2,1)S(1)}, bf16[1,256,4,64]{3,2,1,0:T(4,128)(2,1)}, u32[]{:S(2)}) copy-start(bf16[1,256,4,64]{3,2,1,0:T(4,128)(2,1)} %stack.380) | copy-start | bytes 393220
  168.2 46.1 %copy-start.41 = (bf16[1,256,4,64]{3,2,1,0:T(4,128)(2,1)S(1)}, bf16[1,256,4,64]{3,2,1,0:T(4,128)(2,1)}, u32[]{:S(2)}) copy-start(bf16[1,256,4,64]{3,2,1,0:T(4,128)(2,1)} %stack.381) | copy-start | bytes 393220
  168.2 46.9 %copy-start.39 = (bf16[1,256,4,64]{3,2,1,0:T(4,128)(2,1)S(1)}, bf16[1,256,4,64]{3,2,1,0:T(4,128)(2,1)}, u32[]{:S(2)}) copy-start(bf16[1,256,4,64]{3,2,1,0:T(4,128)(2,1)} %stack.382) | copy-start | bytes 393220
  168.2 47.6 %copy-start.6 = (bf16[1,256,4,64]{3,2,1,0:T(4,128)(2,1)S(1)}, bf16[1,256,4,64]{3,2,1,0:T(4,128)(2,1)}, u32[]{:S(2)}) copy-start(bf16[1,256,4,64]{3,2,1,0:T(4,128)(2,1)} %stack.383) | copy-start | bytes 393220
  168.2 48.4 %copy-start.36 = (bf16[1,256,4,64]{3,2,1,0:T(4,128)(2,1)S(1)}, bf16[1,256,4,64]{3,2,1,0:T(4,128)(2,1)}, u32[]{:S(2)}) copy-start(bf16[1,256,4,64]{3,2,1,0:T(4,128)(2,1)} %stack.384) | copy-start | bytes 393220
  168.2 49.2 %copy-start.35 = (bf16[1,256,4,64]{3,2,1,0:T(4,128)(2,1)S(1)}, bf16[1,256,4,64]{3,2,1,0:T(4,128)(2,1)}, u32[]{:S(2)}) copy-start(bf16[1,256,4,64]{3,2,1,0:T(4,128)(2,1)} %stack.385) | copy-start | bytes 393220
  168.2 50.0 %copy-start.33 = (bf16[1,256,4,64]{3,2,1,0:T(4,128)(2,1)S(1)}, bf16[1,256,4,64]{3,2,1,0:T(4,128)(2,1)}, u32[]{:S(2)}) copy-start(bf16[1,256,4,64]{3,2,1,0:T(4,128)(2,1)} %stack.386) | copy-start | bytes 393220
  168.2 50.8 %copy-start.31 = (bf16[1,256,4,64]{3,2,1,0:T(4,128)(2,1)S(1)}, bf16[1,256,4,64]{3,2,1,0:T(4,128)(2,1)}, u32[]{:S(2)}) copy-start(bf16[1,256,4,64]{3,2,1,0:T(4,128)(2,1)} %stack.387) | copy-start | bytes 393220
  168.2 51.6 %copy-start.29 = (bf16[1,256,4,64]{3,2,1,0:T(4,128)(2,1)S(1)}, bf16[1,256,4,64]{3,2,1,0:T(4,128)(2,1)}, u32[]{:S(2)}) copy-start(bf16[1,256,4,64]{3,2,1,0:T(4,128)(2,1)} %stack.388) | copy-start | bytes 393220
  168.2 52.4 %copy-start.27 = (bf16[1,256,4,64]{3,2,1,0:T(4,128)(2,1)S(1)}, bf16[1,256,4,64]{3,2,1,0:T(4,128)(2,1)}, u32[]{:S(2)}) copy-start(bf16[1,256,4,64]{3,2,1,0:T(4,128)(2,1)} %stack.389) | copy-start | bytes 393220
  168.3 53.2 %copy-start.5 = (bf16[1,256,4,64]{3,2,1,0:T(4,128)(2,1)S(1)}, bf16[1,256,4,64]{3,2,1,0:T(4,128)(2,1)}, u32[]{:S(2)}) copy-start(bf16[1,256,4,64]{3,2,1,0:T(4,128)(2,1)} %stack.390) | copy-start | bytes 393220
  168.3 54.0 %copy-start.24 = (bf16[1,256,4,64]{3,2,1,0:T(4,128)(2,1)S(1)}, bf16[1,256,4,64]{3,2,1,0:T(4,128)(2,1)}, u32[]{:S(2)}) copy-start(bf16[1,256,4,64]{3,2,1,0:T(4,128)(2,1)} %stack.391) | copy-start | bytes 393220
  168.3 54.8 %copy-start.23 = (bf16[1,256,4,64]{3,2,1,0:T(4,128)(2,1)S(1)}, bf16[1,256,4,64]{3,2,1,0:T(4,128)(2,1)}, u32[]{:S(2)}) copy-start(bf16[1,256,4,64]{3,2,1,0:T(4,128)(2,1)} %stack.392) | copy-start | bytes 393220
  168.3 55.6 %copy-start.21 = (bf16[1,256,4,64]{3,2,1,0:T(4,128)(2,1)S(1)}, bf16[1,256,4,64]{3,2,1,0:T(4,128)(2,1)}, u32[]{:S(2)}) copy-start(bf16[1,256,4,64]{3,2,1,0:T(4,128)(2,1)} %stack.393) | copy-start | bytes 393220
  168.3 56.4 %copy-start.19 = (bf16[1,256,4,64]{3,2,1,0:T(4,128)(2,1)S(1)}, bf16[1,256,4,64]{3,2,1,0:T(4,128)(2,1)}, u32[]{:S(2)}) copy-start(bf16[1,256,4,64]{3,2,1,0:T(4,128)(2,1)} %stack.394) | copy-start | bytes 393220
  168.3 57.2 %copy-start.17 = (bf16[1,256,4,64]{3,2,1,0:T(4,128)(2,1)S(1)}, bf16[1,256,4,64]{3,2,1,0:T(4,128)(2,1)}, u32[]{:S(2)}) copy-start(bf16[1,256,4,64]{3,2,1,0:T(4,128)(2,1)} %stack.395) | copy-start | bytes 393220
  168.3 58.0 %copy-start.15 = (bf16[1,256,4,64]{3,2,1,0:T(4,128)(2,1)S(1)}, bf16[1,256,4,64]{3,2,1,0:T(4,128)(2,1)}, u32[]{:S(2)}) copy-start(bf16[1,256,4,64]{3,2,1,0:T(4,128)(2,1)} %stack.396) | copy-start | bytes 393220
  168.3 58.8 %copy-start.4 = (bf16[1,256,4,64]{3,2,1,0:T(4,128)(2,1)S(1)}, bf16[1,256,4,64]{3,2,1,0:T(4,128)(2,1)}, u32[]{:S(2)}) copy-start(bf16[1,256,4,64]{3,2,1,0:T(4,128)(2,1)} %stack.397) | copy-start | bytes 393220
  168.3 59.6 %copy-start.12 = (bf16[1,256,4,64]{3,2,1,0:T(4,128)(2,1)S(1)}, bf16[1,256,4,64]{3,2,1,0:T(4,128)(2,1)}, u32[]{:S(2)}) copy-start(bf16[1,256,4,64]{3,2,1,0:T(4,128)(2,1)} %stack.398) | copy-start | bytes 393220
  168.3 60.4 %copy-start.10 = (bf16[1,256,4,64]{3,2,1,0:T(4,128)(2,1)S(1)}, bf16[1,256,4,64]{3,2,1,0:T(4,128)(2,1)}, u32[]{:S(2)}) copy-start(bf16[1,256,4,64]{3,2,1,0:T(4,128)(2,1)} %stack.399) | copy-start | bytes 393220
  168.4 61.2 %copy-start.7 = (bf16[1,256,4,64]{3,2,1,0:T(4,128)(2,1)S(1)}, bf16[1,256,4,64]{3,2,1,0:T(4,128)(2,1)}, u32[]{:S(2)}) copy-start(bf16[1,256,4,64]{3,2,1,0:T(4,128)(2,1)} %stack.400) | copy-start | bytes 393220
  168.4 62.0 %copy-start.48 = (bf16[256,4,64,1]{2,1,0,3:T(4,128)(2,1)S(1)}, bf16[256,4,64,1]{2,1,0,3:T(4,128)(2,1)}, u32[]{:S(2)}) copy-start(bf16[256,4,64,1]{2,1,0,3:T(4,128)(2,1)} %fusion.22) | copy-start | bytes 393220
  227.1 28.0 %copy-start.50 = (f32[4]{0:T(128)S(1)}, f32[4]{0:T(128)}, u32[]{:S(2)}) copy-start(f32[4]{0:T(128)} %broadcast_multiply_fusion.1) | copy-start | bytes 52
  261.5 104.2 %copy-start.2 = (bf16[1,256,4,64]{3,2,1,0:T(4,128)(2,1)S(1)}, bf16[1,256,4,64]{3,2,1,0:T(4,128)(2,1)}, u32[]{:S(2)}) copy-start(bf16[1,256,4,64]{3,2,1,0:T(4,128)(2,1)} %stack.826) | copy-start | bytes 393220
  337.5 42.0 %copy-start.44 = (bf16[1,256,4,64]{3,2,1,0:T(4,128)(2,1)S(1)}, bf16[1,256,4,64]{3,2,1,0:T(4,128)(2,1)}, u32[]{:S(2)}) copy-start(bf16[1,256,4,64]{3,2,1,0:T(4,128)(2,1)} %stack.835) | copy-start | bytes 393220
  337.5 42.8 %copy-start.42 = (bf16[1,256,4,64]{3,2,1,0:T(4,128)(2,1)S(1)}, bf16[1,256,4,64]{3,2,1,0:T(4,128)(2,1)}, u32[]{:S(2)}) copy-start(bf16[1,256,4,64]{3,2,1,0:T(4,128)(2,1)} %stack.836) | copy-start | bytes 393220
  337.5 43.6 %copy-start.40 = (bf16[1,256,4,64]{3,2,1,0:T(4,128)(2,1)S(1)}, bf16[1,256,4,64]{3,2,1,0:T(4,128)(2,1)}, u32[]{:S(2)}) copy-start(bf16[1,256,4,64]{3,2,1,0:T(4,128)(2,1)} %stack.837) | copy-start | bytes 393220
  337.5 44.5 %copy-start.38 = (bf16[1,256,4,64]{3,2,1,0:T(4,128)(2,1)S(1)}, bf16[1,256,4,64]{3,2,1,0:T(4,128)(2,1)}, u32[]{:S(2)}) copy-start(bf16[1,256,4,64]{3,2,1,0:T(4,128)(2,1)} %stack.838) | copy-start | bytes 393220
  337.5 45.2 %copy-start.37 = (bf16[1,256,4,64]{3,2,1,0:T(4,128)(2,1)S(1)}, bf16[1,256,4,64]{3,2,1,0:T(4,128)(2,1)}, u32[]{:S(2)}) copy-start(bf16[1,256,4,64]{3,2,1,0:T(4,128)(2,1)} %stack.839) | copy-start | bytes 393220
  337.5 46.9 %copy-start.34 = (bf16[1,256,4,64]{3,2,1,0:T(4,128)(2,1)S(1)}, bf16[1,256,4,64]{3,2,1,0:T(4,128)(2,1)}, u32[]{:S(2)}) copy-start(bf16[1,256,4,64]{3,2,1,0:T(4,128)(2,1)} %stack.841) | copy-start | bytes 393220
  337.5 47.6 %copy-start.32 = (bf16[1,256,4,64]{3,2,1,0:T(4,128)(2,1)S(1)}, bf16[1,256,4,64]{3,2,1,0:T(4,128)(2,1)}, u32[]{:S(2)}) copy-start(bf16[1,256,4,64]{3,2,1,0:T(4,128)(2,1)} %stack.842) | copy-start | bytes 393220
  337.5 48.4 %copy-start.30 = (bf16[1,256,4,64]{3,2,1,0:T(4,128)(2,1)S(1)}, bf16[1,256,4,64]{3,2,1,0:T(4,128)(2,1)}, u32[]{:S(2)}) copy-start(bf16[1,256,4,64]{3,2,1,0:T(4,128)(2,1)} %stack.843) | copy-start | bytes 393220
  337.5 49.2 %copy-start.28 = (bf16[1,256,4,64]{3,2,1,0:T(4,128)(2,1)S(1)}, bf16[1,256,4,64]{3,2,1,0:T(4,128)(2,1)}, u32[]{:S(2)}) copy-start(bf16[1,256,4,64]{3,2,1,0:T(4,128)(2,1)} %stack.844) | copy-start | bytes 393220
  337.5 50.0 %copy-start.26 = (bf16[1,256,4,64]{3,2,1,0:T(4,128)(2,1)S(1)}, bf16[1,256,4,64]{3,2,1,0:T(4,128)(2,1)}, u32[]{:S(2)}) copy-start(bf16[1,256,4,64]{3,2,1,0:T(4,128)(2,1)} %stack.845) | copy-start | bytes 393220
  337.5 50.8 %copy-start.25 = (bf16[1,256,4,64]{3,2,1,0:T(4,128)(2,1)S(1)}, bf16[1,256,4,64]{3,2,1,0:T(4,128)(2,1)}, u32[]{:S(2)}) copy-start(bf16[1,256,4,64]{3,2,1,0:T(4,128)(2,1)} %stack.846) | copy-start | bytes 393220
  337.5 52.4 %copy-start.22 = (bf16[1,256,4,64]{3,2,1,0:T(4,128)(2,1)S(1)}, bf16[1,256,4,64]{3,2,1,0:T(4,128)(2,1)}, u32[]{:S(2)}) copy-start(bf16[1,256,4,64]{3,2,1,0:T(4,128)(2,1)} %stack.848) | copy-start | bytes 393220
  337.6 53.2 %copy-start.20 = (bf16[1,256,4,64]{3,2,1,0:T(4,128)(2,1)S(1)}, bf16[1,256,4,64]{3,2,1,0:T(4,128)(2,1)}, u32[]{:S(2)}) copy-start(bf16[1,256,4,64]{3,2,1,0:T(4,128)(2,1)} %stack.849) | copy-start | bytes 393220
  337.6 53.9 %copy-start.18 = (bf16[1,256,4,64]{3,2,1,0:T(4,128)(2,1)S(1)}, bf16[1,256,4,64]{3,2,1,0:T(4,128)(2,1)}, u32[]{:S(2)}) copy-start(bf16[1,256,4,64]{3,2,1,0:T(4,128)(2,1)} %stack.850) | copy-start | bytes 393220
  337.6 54.8 %copy-start.16 = (bf16[1,256,4,64]{3,2,1,0:T(4,128)(2,1)S(1)}, bf16[1,256,4,64]{3,2,1,0:T(4,128)(2,1)}, u32[]{:S(2)}) copy-start(bf16[1,256,4,64]{3,2,1,0:T(4,128)(2,1)} %stack.851) | copy-start | bytes 393220
  337.6 55.6 %copy-start.13 = (bf16[1,256,4,64]{3,2,1,0:T(4,128)(2,1)S(1)}, bf16[1,256,4,64]{3,2,1,0:T(4,128)(2,1)}, u32[]{:S(2)}) copy-start(bf16[1,256,4,64]{3,2,1,0:T(4,128)(2,1)} %stack.852) | copy-start | bytes 393220
  337.6 56.4 %copy-start.14 = (bf16[1,256,4,64]{3,2,1,0:T(4,128)(2,1)S(1)}, bf16[1,256,4,64]{3,2,1,0:T(4,128)(2,1)}, u32[]{:S(2)}) copy-start(bf16[1,256,4,64]{3,2,1,0:T(4,128)(2,1)} %stack.853) | copy-start | bytes 393220
  337.6 58.0 %copy-start.11 = (bf16[1,256,4,64]{3,2,1,0:T(4,128)(2,1)S(1)}, bf16[1,256,4,64]{3,2,1,0:T(4,128)(2,1)}, u32[]{:S(2)}) copy-start(bf16[1,256,4,64]{3,2,1,0:T(4,128)(2,1)} %stack.855) | copy-start | bytes 393220
  337.6 58.8 %copy-start.8 = (bf16[1,256,4,64]{3,2,1,0:T(4,128)(2,1)S(1)}, bf16[1,256,4,64]{3,2,1,0:T(4,128)(2,1)}, u32[]{:S(2)}) copy-start(bf16[1,256,4,64]{3,2,1,0:T(4,128)(2,1)} %stack.856) | copy-start | bytes 393220
  337.6 59.6 %copy-start.9 = (bf16[1,256,4,64]{3,2,1,0:T(4,128)(2,1)S(1)}, bf16[1,256,4,64]{3,2,1,0:T(4,128)(2,1)}, u32[]{:S(2)}) copy-start(bf16[1,256,4,64]{3,2,1,0:T(4,128)(2,1)} %stack.857) | copy-start | bytes 393220
  389.1 27.4 %copy-start.1 = (bf16[16,16,256]{2,1,0:T(8,128)(2,1)S(1)}, bf16[16,16,256]{2,1,0:T(8,128)(2,1)}, u32[]{:S(2)}) copy-start(bf16[16,16,256]{2,1,0:T(8,128)(2,1)} %param.13) | copy-start | bytes 393220
  389.1 27.4 %copy-start.49 = (bf16[256,256]{1,0:T(8,128)(2,1)S(1)}, bf16[256,256]{1,0:T(8,128)(2,1)}, u32[]{:S(2)}) copy-start(bf16[256,256]{1,0:T(8,128)(2,1)} %param.17) | copy-start | bytes 393220
  389.9 27.0 %copy-start.52 = (f32[256]{0:T(256)S(1)}, f32[256]{0:T(256)}, u32[]{:S(2)}) copy-start(f32[256]{0:T(256)} %param.18) | copy-start | bytes 3076
  398.0 22.6 %copy-start.47 = (bf16[256,1024]{1,0:T(8,128)(2,1)S(1)}, bf16[256,1024]{1,0:T(8,128)(2,1)}, u32[]{:S(2)}) copy-start(bf16[256,1024]{1,0:T(8,128)(2,1)} %param.21) | copy-start | bytes 1572868
  398.0 24.0 %copy-start.51 = (f32[1024]{0:T(1024)S(1)}, f32[1024]{0:T(1024)}, u32[]{:S(2)}) copy-start(f32[1024]{0:T(1024)} %param.22) | copy-start | bytes 12292
  416.4 37.4 %copy-start.53 = (f32[16]{0:T(128)S(1)}, f32[16]{0:T(128)}, u32[]{:S(2)}) copy-start(f32[16]{0:T(128)} %param.24) | copy-start | bytes 196
  438.8 46.7 %all-to-all-start = ((bf16[256,2,1024]{2,1,0:T(2,128)(2,1)}), bf16[256,2,1024]{2,1,0:T(2,128)(2,1)S(1)}, u32[]{:S(2)}, u32[]{:S(2)}) async-start(bf16[256,2,1024]{2,1,0:T(2,128)(2,1)} %reshape.621), calls=%async_computation | async-start | bytes 2097152 | tf_op jit(solution)/shard_map/all_to_all | solution.py:133
